TPU v7x, 32 devices: a whole 2x2x4 slice. The times are simulated.
32 devices in a mesh: shard: 4 (over z), context: 2 (over y), tensor: 4 (over x, core).
Axes of the slice: x: 2, y: 2, z: 4, core: 2. Of those that a mesh axis runs over, the one named last changes fastest.
Arguments:
- tokens: bfloat16 [16, 1024, 1024], P('shard', 'context'), may hold values from -6 to 6
- cotangent: bfloat16 [16, 1024, 1024], P('shard', 'context'), may hold values from -6 to 6
- adapter_index: int32 [16], P('shard'), may hold values from 0 to 7, as said below
- ln1_gain: float32 [1024], replicated, may hold values from 0.5 to 1.5
- ln1_bias: float32 [1024], replicated, may hold values from -1.5 to 1.5
- ln2_gain: float32 [1024], replicated, may hold values from 0.5 to 1.5
- ln2_bias: float32 [1024], replicated, may hold values from -1.5 to 1.5
- layer_scale: float32 [2, 1024], replicated, may hold values from 0.4 to 1.2
- w_qkv: bfloat16 [1024, 3, 1024], P(('shard', 'context'), None, 'tensor'), may hold values from -0.1875 to 0.1875
- w_proj: bfloat16 [1024, 1024], P(('shard', 'context'), 'tensor'), may hold values from -0.5 to 0.5
- w_fc1: bfloat16 [1024, 4096], P(('shard', 'context'), 'tensor'), may hold values from -0.1875 to 0.1875
- w_fc2: bfloat16 [1024, 4096], P(('shard', 'context'), 'tensor'), may hold values from -0.09375 to 0.09375
- down_in: bfloat16 [8, 4, 1024, 16], replicated, may hold values from -0.1875 to 0.1875
- qkv_up: bfloat16 [8, 3, 16, 1024], P(None, None, None, 'tensor'), may hold values from -1.5 to 1.5
- fc1_up: bfloat16 [8, 16, 4096], P(None, None, 'tensor'), may hold values from -1.5 to 1.5
- proj_down: bfloat16 [8, 1024, 16], P(None, 'tensor'), may hold values from -0.5 to 0.5
- fc2_down: bfloat16 [8, 4096, 16], P(None, 'tensor'), may hold values from -0.09375 to 0.09375
- out_up: bfloat16 [8, 2, 16, 1024], replicated, may hold values from -1.5 to 1.5
Outputs:
- result: bfloat16 [16, 1024, 1024], P('shard', 'context')
- input_grad: float32 [16, 1024, 1024], P('shard', 'context')
- down_in_grad: float32 [8, 4, 1024, 16], replicated
- qkv_up_grad: float32 [8, 3, 16, 1024], P(None, None, None, 'tensor')
- fc1_up_grad: float32 [8, 16, 4096], P(None, None, 'tensor')
- proj_down_grad: float32 [8, 1024, 16], P(None, 'tensor')
- fc2_down_grad: float32 [8, 4096, 16], P(None, 'tensor')
- out_up_grad: float32 [8, 2, 16, 1024], replicated
Inputs may be any that keep to these rules, and one draw needn't show every extreme that they name: `adapter_index`: every adapter index is used by exactly 2 images.
All inputs are finite; a program needn't handle non-finite values.
Results may differ from a plain program's by a relative error of at most 0.015.
The roundings to bfloat16 on the way count: a program that leaves them out, or rounds other values in their place, can miss the bound.
Values may be sent and summed in bfloat16 or wider, within the bound.
No kernel may reach another device: no remote copies, remote signals or barrier semaphores. Data moves between devices by JAX's collectives and lax.ppermute only.
A program may use at most 256 MiB of HBM per device.

v0:
```python
import math

import jax
import jax.numpy as jnp
from jax import lax
from jax.sharding import PartitionSpec as P

HEAD_DIM = 64


eps_norm = 1e-06


def normalize(values, norm_gain, norm_shift):
    centre = values - jnp.mean(values, axis=-1, keepdims=True)
    inverse = lax.rsqrt(jnp.mean(centre * centre, axis=-1, keepdims=True) + eps_norm)
    unit_values = centre * inverse
    return (unit_values * norm_gain + norm_shift, unit_values, inverse)


def norm_back(grad_out, unit_values, inverse, norm_gain):
    scaled = grad_out * norm_gain
    centred = scaled - jnp.mean(scaled, axis=-1, keepdims=True)
    return inverse * (
        centred - unit_values * jnp.mean(scaled * unit_values, axis=-1, keepdims=True)
    )


def per_device(
    tokens,
    cotangent,
    adapter_index,
    ln1_gain,
    ln1_bias,
    ln2_gain,
    ln2_bias,
    layer_scale,
    w_qkv,
    w_proj,
    w_fc1,
    w_fc2,
    down_in,
    qkv_up,
    fc1_up,
    proj_down,
    fc2_down,
    out_up,
):
    images, row_count, model_width = tokens.shape
    adapter_count = down_in.shape[0]
    choose = (adapter_index[:, None] == jnp.arange(adapter_count, dtype=jnp.int32)[None, :]).astype(
        jnp.bfloat16
    )
    choose_float = choose.astype(jnp.float32)

    def select_rows(stacked):
        return jnp.einsum(
            "ia,a...->i...", choose, stacked, preferred_element_type=jnp.float32
        ).astype(jnp.bfloat16)

    def collect(per_image):
        return jnp.einsum("ia,i...->a...", choose_float, per_image, precision=lax.Precision.HIGHEST)

    sel_down = select_rows(down_in)
    sel_qkv = select_rows(qkv_up)
    sel_fc1 = select_rows(fc1_up)
    sel_proj = select_rows(proj_down)
    sel_fc2 = select_rows(fc2_down)
    sel_out = select_rows(out_up)
    score_scale = 1.0 / math.sqrt(HEAD_DIM)
    attn_full, proj_full = (
        lax.all_gather(w_qkv, ("shard", "context"), axis=0, tiled=True),
        lax.all_gather(w_proj, ("shard", "context"), axis=0, tiled=True),
    )
    fc1_full, fc2_full = (
        lax.all_gather(w_fc1, ("shard", "context"), axis=0, tiled=True),
        lax.all_gather(w_fc2, ("shard", "context"), axis=0, tiled=True),
    )
    resid = tokens.astype(jnp.float32)
    normed, unit_one, inverse_one = normalize(resid, ln1_gain, ln1_bias)
    normed_low = normed.astype(jnp.bfloat16)
    rank_qkv = jnp.einsum(
        "ild,ikdr->iklr", normed_low, sel_down[:, :3], preferred_element_type=jnp.float32
    ).astype(jnp.bfloat16)
    projected = jnp.einsum(
        "ild,dkc->iklc", normed_low, attn_full, preferred_element_type=jnp.float32
    )
    projected = projected + jnp.einsum(
        "iklr,ikrc->iklc", rank_qkv, sel_qkv, preferred_element_type=jnp.float32
    )
    projected_low = projected.astype(jnp.bfloat16)
    local_width = projected_low.shape[-1]
    head_count = local_width // HEAD_DIM
    queries = projected_low[:, 0].reshape(images, row_count, head_count, HEAD_DIM)
    keys_all, values_all = (
        lax.all_gather(projected_low[:, 1], "context", axis=1, tiled=True),
        lax.all_gather(projected_low[:, 2], "context", axis=1, tiled=True),
    )
    key_heads = keys_all.reshape(images, -1, head_count, HEAD_DIM)
    value_heads = values_all.reshape(images, -1, head_count, HEAD_DIM)
    scores = (
        jnp.einsum("iqhe,ikhe->ihqk", queries, key_heads, preferred_element_type=jnp.float32)
        * score_scale
    )
    row_peak = jnp.max(scores, axis=-1, keepdims=True)
    exp_scores = jnp.exp(scores - row_peak)
    exp_total = jnp.sum(exp_scores, axis=-1, keepdims=True)
    log_total = row_peak + jnp.log(exp_total)
    probabilities = (exp_scores / exp_total).astype(jnp.bfloat16)
    mixed_heads = jnp.einsum(
        "ihqk,ikhe->iqhe", probabilities, value_heads, preferred_element_type=jnp.float32
    )
    mixed_low = mixed_heads.reshape(images, row_count, local_width).astype(jnp.bfloat16)
    proj_part = jnp.einsum("ilc,dc->ild", mixed_low, proj_full, preferred_element_type=jnp.float32)
    proj_rank_part = jnp.einsum(
        "ilc,icr->ilr", mixed_low, sel_proj, preferred_element_type=jnp.float32
    )
    proj_total, proj_rank_total = lax.psum((proj_part, proj_rank_part), "tensor")
    proj_rank = proj_rank_total.astype(jnp.bfloat16)
    attn_out = proj_total + jnp.einsum(
        "ilr,ird->ild", proj_rank, sel_out[:, 0], preferred_element_type=jnp.float32
    )
    hidden_one = resid + layer_scale[0] * attn_out
    normed_two, unit_two, inverse_two = normalize(hidden_one, ln2_gain, ln2_bias)
    normed_two_low = normed_two.astype(jnp.bfloat16)
    fc1_rank = jnp.einsum(
        "ild,idr->ilr", normed_two_low, sel_down[:, 3], preferred_element_type=jnp.float32
    ).astype(jnp.bfloat16)
    preact = jnp.einsum("ild,df->ilf", normed_two_low, fc1_full, preferred_element_type=jnp.float32)
    preact = preact + jnp.einsum(
        "ilr,irf->ilf", fc1_rank, sel_fc1, preferred_element_type=jnp.float32
    )
    activation = jax.nn.gelu(preact, approximate=False).astype(jnp.bfloat16)
    mlp_part = jnp.einsum("ilf,df->ild", activation, fc2_full, preferred_element_type=jnp.float32)
    fc2_rank_part = jnp.einsum(
        "ilf,ifr->ilr", activation, sel_fc2, preferred_element_type=jnp.float32
    )
    mlp_total, fc2_rank_total = (
        lax.psum(mlp_part.astype(jnp.bfloat16), "tensor").astype(jnp.float32),
        lax.psum(fc2_rank_part.astype(jnp.bfloat16), "tensor").astype(jnp.float32),
    )
    fc2_rank = fc2_rank_total.astype(jnp.bfloat16)
    branch = mlp_total + jnp.einsum(
        "ilr,ird->ild", fc2_rank, sel_out[:, 1], preferred_element_type=jnp.float32
    )
    result = (hidden_one + layer_scale[1] * branch).astype(jnp.bfloat16)
    upstream = cotangent.astype(jnp.float32)
    fc1_back, fc2_back = (
        lax.all_gather(w_fc1, ("shard", "context"), axis=0, tiled=True),
        lax.all_gather(w_fc2, ("shard", "context"), axis=0, tiled=True),
    )
    grad_branch = (upstream * layer_scale[1]).astype(jnp.bfloat16)
    grad_fc2_rank = jnp.einsum(
        "ild,ird->ilr", grad_branch, sel_out[:, 1], preferred_element_type=jnp.float32
    ).astype(jnp.bfloat16)
    out_grad_fc2 = jnp.einsum(
        "ilr,ild->ird", fc2_rank, grad_branch, preferred_element_type=jnp.float32
    )
    grad_activation = jnp.einsum(
        "ild,df->ilf", grad_branch, fc2_back, preferred_element_type=jnp.float32
    )
    grad_activation = grad_activation + jnp.einsum(
        "ilr,ifr->ilf", grad_fc2_rank, sel_fc2, preferred_element_type=jnp.float32
    )
    fc2_down_part = jnp.einsum(
        "ilf,ilr->ifr", activation, grad_fc2_rank, preferred_element_type=jnp.float32
    )
    normal_cdf = 0.5 * (1.0 + lax.erf(preact * (1.0 / math.sqrt(2.0))))
    normal_density = jnp.exp(-0.5 * preact * preact) * (1.0 / math.sqrt(2.0 * math.pi))
    grad_preact = (grad_activation * (normal_cdf + preact * normal_density)).astype(jnp.bfloat16)
    fc1_up_part = jnp.einsum(
        "ilr,ilf->irf", fc1_rank, grad_preact, preferred_element_type=jnp.float32
    )
    normed_two_part = jnp.einsum(
        "ilf,df->ild", grad_preact, fc1_back, preferred_element_type=jnp.float32
    )
    fc1_rank_part = jnp.einsum(
        "ilf,irf->ilr", grad_preact, sel_fc1, preferred_element_type=jnp.float32
    )
    grad_normed_two, grad_fc1_total = lax.psum((normed_two_part, fc1_rank_part), "tensor")
    grad_fc1_rank = grad_fc1_total.astype(jnp.bfloat16)
    grad_normed_two = grad_normed_two + jnp.einsum(
        "ilr,idr->ild", grad_fc1_rank, sel_down[:, 3], preferred_element_type=jnp.float32
    )
    fc1_down_part = jnp.einsum(
        "ild,ilr->idr", normed_two_low, grad_fc1_rank, preferred_element_type=jnp.float32
    )
    grad_hidden = upstream + norm_back(grad_normed_two, unit_two, inverse_two, ln2_gain)
    qkv_back, proj_back = (
        lax.all_gather(w_qkv, ("shard", "context"), axis=0, tiled=True),
        lax.all_gather(w_proj, ("shard", "context"), axis=0, tiled=True),
    )
    grad_attn = (grad_hidden * layer_scale[0]).astype(jnp.bfloat16)
    grad_proj_rank = jnp.einsum(
        "ild,ird->ilr", grad_attn, sel_out[:, 0], preferred_element_type=jnp.float32
    ).astype(jnp.bfloat16)
    out_grad_proj = jnp.einsum(
        "ilr,ild->ird", proj_rank, grad_attn, preferred_element_type=jnp.float32
    )
    grad_mixed = jnp.einsum("ild,dc->ilc", grad_attn, proj_back, preferred_element_type=jnp.float32)
    grad_mixed = grad_mixed + jnp.einsum(
        "ilr,icr->ilc", grad_proj_rank, sel_proj, preferred_element_type=jnp.float32
    )
    grad_mixed_low = grad_mixed.astype(jnp.bfloat16)
    proj_down_part = jnp.einsum(
        "ilc,ilr->icr", mixed_low, grad_proj_rank, preferred_element_type=jnp.float32
    )
    keys_back, values_back = (keys_all, values_all)
    key_heads_back = keys_back.reshape(images, -1, head_count, HEAD_DIM)
    value_heads_back = values_back.reshape(images, -1, head_count, HEAD_DIM)
    grad_heads = grad_mixed_low.reshape(images, row_count, head_count, HEAD_DIM)
    scores_again = (
        jnp.einsum("iqhe,ikhe->ihqk", queries, key_heads_back, preferred_element_type=jnp.float32)
        * score_scale
    )
    probs_again = jnp.exp(scores_again - log_total)
    grad_probs = jnp.einsum(
        "iqhe,ikhe->ihqk", grad_heads, value_heads_back, preferred_element_type=jnp.float32
    )
    row_inner = jnp.sum(probs_again * grad_probs, axis=-1, keepdims=True)
    grad_scores = (probs_again * (grad_probs - row_inner)).astype(jnp.bfloat16)
    grad_queries = (
        jnp.einsum(
            "ihqk,ikhe->iqhe", grad_scores, key_heads_back, preferred_element_type=jnp.float32
        )
        * score_scale
    )
    key_part = (
        jnp.einsum("ihqk,iqhe->ikhe", grad_scores, queries, preferred_element_type=jnp.float32)
        * score_scale
    )
    value_part = jnp.einsum(
        "ihqk,iqhe->ikhe",
        probs_again.astype(jnp.bfloat16),
        grad_heads,
        preferred_element_type=jnp.float32,
    )
    key_grad, value_grad = (
        lax.psum_scatter(
            key_part.reshape(images, -1, local_width), "context", scatter_dimension=1, tiled=True
        ),
        lax.psum_scatter(
            value_part.reshape(images, -1, local_width), "context", scatter_dimension=1, tiled=True
        ),
    )
    grad_projected = jnp.stack(
        [grad_queries.reshape(images, row_count, local_width), key_grad, value_grad], axis=1
    ).astype(jnp.bfloat16)
    qkv_up_part = jnp.einsum(
        "iklr,iklc->ikrc", rank_qkv, grad_projected, preferred_element_type=jnp.float32
    )
    normed_part = jnp.einsum(
        "iklc,dkc->ild", grad_projected, qkv_back, preferred_element_type=jnp.float32
    )
    rank_part = jnp.einsum(
        "iklc,ikrc->iklr", grad_projected, sel_qkv, preferred_element_type=jnp.float32
    )
    grad_normed, grad_rank_total = lax.psum((normed_part, rank_part), "tensor")
    grad_rank = grad_rank_total.astype(jnp.bfloat16)
    grad_normed = grad_normed + jnp.einsum(
        "iklr,ikdr->ild", grad_rank, sel_down[:, :3], preferred_element_type=jnp.float32
    )
    qkv_down_part = jnp.einsum(
        "ild,iklr->ikdr", normed_low, grad_rank, preferred_element_type=jnp.float32
    )
    input_grad = grad_hidden + norm_back(grad_normed, unit_one, inverse_one, ln1_gain)
    down_total = collect(jnp.concatenate([qkv_down_part, fc1_down_part[:, None]], axis=1))
    qkv_up_total = collect(qkv_up_part)
    fc1_up_total = collect(fc1_up_part)
    proj_down_total = collect(proj_down_part)
    fc2_down_total = collect(fc2_down_part)
    out_up_total = collect(jnp.stack([out_grad_proj, out_grad_fc2], axis=1))
    adapter_sums = lax.psum(
        (down_total, qkv_up_total, fc1_up_total, proj_down_total, fc2_down_total, out_up_total),
        ("shard", "context"),
    )
    return (
        result,
        input_grad,
        adapter_sums[0],
        adapter_sums[1],
        adapter_sums[2],
        adapter_sums[3],
        adapter_sums[4],
        adapter_sums[5],
    )


def solution(mesh):
    placed = (
        P("shard", "context", None),
        P("shard", "context", None),
        P("shard"),
        P(),
        P(),
        P(),
        P(),
        P(),
        P(("shard", "context"), None, "tensor"),
        P(("shard", "context"), "tensor"),
        P(("shard", "context"), "tensor"),
        P(("shard", "context"), "tensor"),
        P(),
        P(None, None, None, "tensor"),
        P(None, None, "tensor"),
        P(None, "tensor", None),
        P(None, "tensor", None),
        P(),
    )
    return jax.shard_map(
        per_device,
        mesh=mesh,
        in_specs=placed,
        out_specs=(
            P("shard", "context", None),
            P("shard", "context", None),
            P(),
            P(None, None, None, "tensor"),
            P(None, None, "tensor"),
            P(None, "tensor", None),
            P(None, "tensor", None),
            P(),
        ),
        check_vma=False,
    )
```

profile of v0, /device:TPU:1, one launch (start us, length us, event | category | flops | bytes accessed | tf_op | source)
XLA Modules:
  0.0 1194.0 jit_solution(3190369262834206231)
XLA Ops:
  17.8 37.4 %all-gather.8.cloned.1.call-done = bf16[1024,3,256]{0,2,1:T(8,128)(2,1)} async-done(((bf16[128,3,256]{0,2,1:T(8,128)(2,1)}), bf16[1024,3,256]{0,2,1:T(8,128)(2,1)}) %all-gather.8.cloned.1.call-update) | async-done | bytes 1572880 | tf_op jit(solution)/shard_map/all_gather | solution.py:72
  65.5 26.2 %all_gather.25 = bf16[1024,256]{1,0:T(8,128)(2,1)S(1)} all-gather(bf16[128,256]{1,0:T(8,128)(2,1)S(1)} %copy-done.55), channel_id=1, replica_groups=mesh['shard'=4,'context'=2,'tensor'=4] {'shard','context'}, dimensions={0}, use_global_device_ids=true | all-gather | bytes 589824 | tf_op jit(solution)/shard_map/all_gather | solution.py:73
  91.6 14.0 %all-gather.16.cloned.1.call-done = bf16[4,1,1024,256]{2,3,1,0:T(8,128)(2,1)} async-done(((bf16[4,1,512,256]{2,3,1,0:T(8,128)(2,1)}), bf16[4,1,1024,256]{2,3,1,0:T(8,128)(2,1)}) %all-gather.16.cloned.1.call-update) | async-done | bytes 2097168 | tf_op jit(solution)/shard_map/all_gather | solution.py:96
  105.6 15.7 %multiply_reduce_fusion.1 = (f32[4,4,512]{2,1,0:T(4,128)S(1)}, f32[4,4,512,1024]{3,2,1,0:T(8,128)}) fusion(bf16[4,512,4,64]{1,3,2,0:T(8,128)(2,1)S(1)} %bitcast.147, bf16[4,1024,4,64]{1,3,2,0:T(8,128)(2,1)} %bitcast.149), kind=kOutput, calls=%fused_computation.6 | convolution fusion | flops 1090510848 | bytes 36732928 | tf_op jit(solution)/shard_map/iqhe,ikhe->ihqk/dot_general | solution.py:102
  121.3 14.2 %fusion = f32[4,4,512]{2,1,0:T(4,128)S(1)} fusion(f32[4,4,512,1024]{3,2,1,0:T(8,128)} %get-tuple-element.38, f32[4,4,512]{2,1,0:T(4,128)S(1)} %get-tuple-element.37), kind=kLoop, calls=%fused_computation.5 | loop fusion | flops 25157632 | bytes 33619968 | tf_op jit(solution)/shard_map/reduce_sum | solution.py:107
  140.3 14.4 %fusion.55 = bf16[4,4,64,512]{3,2,1,0:T(8,128)(2,1)S(1)} fusion(bf16[4,1024,4,64]{1,3,2,0:T(8,128)(2,1)} %bitcast.153, f32[4,4,512,1024]{3,2,1,0:T(8,128)} %get-tuple-element.38, f32[4,4,512]{2,1,0:T(4,128)S(1)} %fusion, f32[4,4,512]{2,1,0:T(4,128)S(1)} %get-tuple-element.37), kind=kOutput, calls=%fused_computation.92 | convolution fusion | flops 1107820544 | bytes 36765696 | tf_op jit(solution)/shard_map/ihqk,ikhe->iqhe/dot_general | solution.py:110
  166.2 23.5 %all-gather.12.cloned.1.call-done = bf16[1024,1024]{1,0:T(8,128)(2,1)} async-done(((bf16[128,1024]{1,0:T(8,128)(2,1)}), bf16[1024,1024]{1,0:T(8,128)(2,1)}) %all-gather.12.cloned.1.call-update) | async-done | bytes 2097168 | tf_op jit(solution)/shard_map/all_gather | solution.py:77
  189.6 11.0 fusion.42
  200.9 17.3 %all-reduce.20 = bf16[4,512,16]{1,2,0:T(8,128)(2,1)S(1)} all-reduce(f32[4,512,16]{1,2,0:T(8,128)S(1)} %fusion.110), channel_id=1, replica_groups=mesh['shard'=4,'context'=2,'tensor'=4] {'tensor'}, use_global_device_ids=true, to_apply=%region_5.0 | all-reduce | flops 32768 | bytes 196608 | tf_op jit(solution)/shard_map/psum | solution.py:118
  218.2 129.5 %all-reduce.11.cloned.1.call-done = f32[4,512,1024]{2,1,0:T(8,128)} async-done(((f32[4,512,1024]{2,1,0:T(8,128)}), f32[4,512,1024]{2,1,0:T(8,128)}) %all-reduce.11.cloned.1.call-update) | async-done | bytes 8388624 | tf_op jit(solution)/shard_map/psum | solution.py:118
  360.7 36.6 %all-gather.10.cloned.1.call-done = bf16[1024,1024]{1,0:T(8,128)(2,1)} async-done(((bf16[128,1024]{1,0:T(8,128)(2,1)}), bf16[1024,1024]{1,0:T(8,128)(2,1)}) %all-gather.10.cloned.1.call-update) | async-done | bytes 2097168 | tf_op jit(solution)/shard_map/all_gather | solution.py:76
  431.8 17.4 %all-reduce.21 = bf16[4,512,16]{1,2,0:T(8,128)(2,1)S(1)} all-reduce(f32[4,512,16]{1,2,0:T(8,128)S(1)} %fusion.89), channel_id=1, replica_groups=mesh['shard'=4,'context'=2,'tensor'=4] {'tensor'}, use_global_device_ids=true, to_apply=%region_11.0 | all-reduce | flops 32768 | bytes 196608 | tf_op jit(solution)/shard_map/psum | solution.py:180
  449.2 134.0 %all-reduce.13.cloned.1.call-done = f32[4,512,1024]{2,1,0:T(8,128)} async-done(((f32[4,512,1024]{2,1,0:T(8,128)}), f32[4,512,1024]{2,1,0:T(8,128)}) %all-reduce.13.cloned.1.call-update) | async-done | bytes 8388624 | tf_op jit(solution)/shard_map/psum | solution.py:180
  602.6 15.4 %fusion.2 = f32[4,4,64,1024]{3,2,1,0:T(8,128)} fusion(bf16[4,512,4,64]{1,3,2,0:T(8,128)(2,1)S(1)} %bitcast.145, f32[4,4,512,1024]{3,2,1,0:T(8,128)} %get-tuple-element.38, f32[4,4,512]{2,1,0:T(4,128)S(1)} %bitcast.155), kind=kOutput, calls=%fused_computation.8 | convolution fusion | flops 1098907648 | bytes 38830080 | tf_op jit(solution)/shard_map/ihqk,iqhe->ikhe/dot_general | solution.py:232
  623.7 22.9 %multiply_reduce_fusion = (f32[4,4,512]{2,1,0:T(4,128)S(1)}, f32[4,4,512,1024]{3,2,1,0:T(8,128)}) fusion(f32[4,4,512,1024]{3,2,1,0:T(8,128)} %get-tuple-element.38, f32[4,4,512]{2,1,0:T(4,128)S(1)} %bitcast.156, bf16[4,512,4,64]{1,3,2,0:T(8,128)(2,1)S(1)} %bitcast.146, bf16[4,1024,4,64]{1,3,2,0:T(8,128)(2,1)S(1)} %bitcast.154), kind=kOutput, calls=%fused_computation.1 | convolution fusion | flops 1107288064 | bytes 70320128 | tf_op jit(solution)/shard_map/iqhe,ikhe->ihqk/dot_general | solution.py:217
  646.6 28.5 %multiply_convert_fusion = bf16[4,4,512,1024]{3,2,1,0:T(8,128)(2,1)} fusion(f32[4,4,512,1024]{3,2,1,0:T(8,128)} %get-tuple-element.44, f32[4,4,512,1024]{3,2,1,0:T(8,128)} %get-tuple-element.38, f32[4,4,512]{2,1,0:T(4,128)S(1)} %get-tuple-element.43, f32[4,4,512]{2,1,0:T(4,128)S(1)} %bitcast.157), kind=kLoop, calls=%fused_computation | loop fusion | flops 41943040 | bytes 83951616 | tf_op jit(solution)/shard_map/convert_element_type | solution.py:221
  675.1 10.9 broadcast_multiply_fusion
  695.3 20.4 %fusion.22 = bf16[4,512,1024]{2,1,0:T(8,128)(2,1)S(1)} fusion(f32[4,512,1024]{2,1,0:T(8,128)} %copy-done.17, u8[512,1024]{1,0:T(8,128)(4,1)S(1)} %copy-done.31, u8[512,1024]{1,0:T(8,128)(4,1)S(1)} %copy-done.30), kind=kLoop, calls=%fused_computation.34 | loop fusion | flops 146800640 | bytes 13631488 | tf_op jit(solution)/shard_map/convert_element_type | solution.py:133
  725.7 11.0 multiply_convert_fusion.2
  763.4 72.2 %all-reduce.19.cloned.1.call-done = (bf16[4,512,1024]{2,1,0:T(8,128)(2,1)}, bf16[4,512,16]{1,2,0:T(8,128)(2,1)}) async-done(((bf16[4,512,1024]{2,1,0:T(8,128)(2,1)}, bf16[4,512,16]{1,2,0:T(8,128)(2,1)}), (bf16[4,512,1024]{2,1,0:T(8,128)(2,1)}, bf16[4,512,16]{1,2,0:T(8,128)(2,1)})) %all-reduce.19.cloned.1.call-update) | async-done | bytes 4259856 | tf_op jit(solution)/shard_map/psum | solution.py:139
  847.5 21.9 %all-reduce.22 = bf16[4,3,512,16]{2,3,1,0:T(8,128)(2,1)S(1)} all-reduce(f32[4,3,512,16]{2,3,1,0:T(8,128)S(1)} %fusion.99), channel_id=1, replica_groups=mesh['shard'=4,'context'=2,'tensor'=4] {'tensor'}, use_global_device_ids=true, to_apply=%region_18.0 | all-reduce | flops 98304 | bytes 589824 | tf_op jit(solution)/shard_map/psum | solution.py:258
  887.2 110.4 %all-reduce.15.cloned.1.call-done = f32[4,512,1024]{2,1,0:T(8,128)} async-done(((f32[4,512,1024]{2,1,0:T(8,128)}), f32[4,512,1024]{2,1,0:T(8,128)}) %all-reduce.15.cloned.1.call-update) | async-done | bytes 8388624 | tf_op jit(solution)/shard_map/psum | solution.py:258
  1004.6 13.0 %fusion.17 = f32[4,512,1024]{2,1,0:T(8,128)} fusion(bf16[4,512,1024]{2,1,0:T(8,128)(2,1)S(1)} %copy-done.4, f32[4,512,1024]{2,1,0:T(8,128)S(1)} %get-tuple-element.45, f32[4,512]{1,0:T(4,128)S(1)} %broadcast_multiply_fusion.1, f32[4,512]{1,0:T(4,128)S(1)} %broadcast_multiply_fusion.2, f32[4,512]{1,0:T(4,128)S(1)} %copy-done.37, f32[4,512]{1,0:T(4,128)S(1)} %copy-done.33, ...), kind=kLoop, calls=%fused_computation.29 | loop fusion | flops 33554432 | bytes 42008576 | tf_op jit(solution)/shard_map/add | solution.py:266
  1017.6 154.6 %all-reduce.17.cloned.1.call-done = (f32[8,4,1024,16]{2,0,3,1:T(8,128)}, f32[8,3,16,256]{3,0,2,1:T(8,128)}, f32[8,16,1024]{2,0,1:T(8,128)}, f32[8,256,16]{1,0,2:...) async-done(((f32[8,4,1024,16]{2,0,3,1:T(8,128)}, f32[8,3,16,256]{3,0,2,1:T(8,128)}, f32[8,16,1024]{2,0,1:T(8,128)}, f32[8,256,16]{1,0,2:T(8,128)}, ...) | async-done | bytes 4718608 | tf_op jit(solution)/shard_map/psum | solution.py:273
  (243 shorter events, 206.4 us)
Async XLA Ops:
  7.2 48.0 %all-gather.8.cloned.1.call-start = ((), (), s32[]{:S(2)}) async-start(), calls=%async_computation.2 | async-start | bytes 1769472 | tf_op jit(solution)/shard_map/all_gather | solution.py:72
  9.1 96.5 %all-gather.16.cloned.1.call-start = ((), (), s32[]{:S(2)}) async-start(), calls=%async_computation.11 | async-start | bytes 3145728 | tf_op jit(solution)/shard_map/all_gather | solution.py:96
  64.1 76.2 %all-gather.14.cloned.1.call-start = ((), (), s32[]{:S(2)}) async-start(), calls=%async_computation.10 | async-start | bytes 3145728 | tf_op jit(solution)/shard_map/all_gather | solution.py:97
  64.8 124.8 %all-gather.12.cloned.1.call-start = ((), (), s32[]{:S(2)}) async-start(), calls=%async_computation.5 | async-start | bytes 2359296 | tf_op jit(solution)/shard_map/all_gather | solution.py:77
  65.4 282.3 %all-reduce.11.cloned.1.call-start = ((), (), s32[]{:S(2)}) async-start(), calls=%async_computation.3 | async-start | bytes 16777216 | tf_op jit(solution)/shard_map/psum | solution.py:118
  159.5 237.8 %all-gather.10.cloned.1.call-start = ((), (), s32[]{:S(2)}) async-start(), calls=%async_computation.4 | async-start | bytes 2359296 | tf_op jit(solution)/shard_map/all_gather | solution.py:76
  160.1 423.1 %all-reduce.13.cloned.1.call-start = ((), (), s32[]{:S(2)}) async-start(), calls=%async_computation.6 | async-start | bytes 16777216 | tf_op jit(solution)/shard_map/psum | solution.py:180
  166.2 243.6 %copy-start.47 = (bf16[4,512,16]{1,2,0:T(8,128)(2,1)}, bf16[4,512,16]{1,2,0:T(8,128)(2,1)S(1)}, u32[]{:S(2)}) copy-start(bf16[4,512,16]{1,2,0:T(8,128)(2,1)S(1)} %fusion.59) | copy-start | bytes 196612
  218.2 135.9 %copy-start.25 = (bf16[4,512,16]{1,2,0:T(8,128)(2,1)}, bf16[4,512,16]{1,2,0:T(8,128)(2,1)S(1)}, u32[]{:S(2)}) copy-start(bf16[4,512,16]{1,2,0:T(8,128)(2,1)S(1)} %all-reduce.20) | copy-start | bytes 196612
  354.1 236.5 %copy-start.38 = (f32[4,512]{1,0:T(4,128)}, f32[4,512]{1,0:T(4,128)S(1)}, u32[]{:S(2)}) copy-start(f32[4,512]{1,0:T(4,128)S(1)} %broadcast_multiply_fusion.5) | copy-start | bytes 24580
  355.3 235.3 %copy-start.42 = (f32[4,512]{1,0:T(4,128)}, f32[4,512]{1,0:T(4,128)S(1)}, u32[]{:S(2)}) copy-start(f32[4,512]{1,0:T(4,128)S(1)} %add_rsqrt_fusion) | copy-start | bytes 24580
  427.9 310.2 %reduce-scatter.5.cloned.1.call-start = ((), (), s32[]{:S(2)}) async-start(), calls=%async_computation.8 | async-start | bytes 6291456 | tf_op jit(solution)/shard_map/reduce_scatter | solution.py:242
  623.5 122.8 %reduce-scatter.3.cloned.1.call-start = ((), (), s32[]{:S(2)}) async-start(), calls=%async_computation.7 | async-start | bytes 6291456 | tf_op jit(solution)/shard_map/reduce_scatter | solution.py:239
  691.5 144.2 %all-reduce.19.cloned.1.call-start = ((), (), s32[]{:S(2)}) async-start(), calls=%async_computation.13 | async-start | bytes 8519680 | tf_op jit(solution)/shard_map/psum | solution.py:139
  725.2 272.4 %all-reduce.15.cloned.1.call-start = ((), (), s32[]{:S(2)}) async-start(), calls=%async_computation.9 | async-start | bytes 16777216 | tf_op jit(solution)/shard_map/psum | solution.py:258
  756.8 415.4 %all-reduce.17.cloned.1.call-start = ((), (), s32[]{:S(2)}) async-start(), calls=%async_computation.12 | async-start | bytes 9437184 | tf_op jit(solution)/shard_map/psum | solution.py:273
  759.0 82.7 %copy-start.14 = (bf16[4,4,64,512]{3,2,1,0:T(8,128)(2,1)S(1)}, bf16[4,4,64,512]{3,2,1,0:T(8,128)(2,1)}, u32[]{:S(2)}) copy-start(bf16[4,4,64,512]{3,2,1,0:T(8,128)(2,1)} %copy-done.13) | copy-start | bytes 3145732
  878.6 119.0 %copy-start.21 = (bf16[4,3,1024,16]{2,0,3,1:T(4,128)(2,1)S(1)}, bf16[4,3,1024,16]{2,0,3,1:T(4,128)(2,1)}, u32[]{:S(2)}) copy-start(bf16[4,3,1024,16]{2,0,3,1:T(4,128)(2,1)} %copy-done.20) | copy-start | bytes 1179652
  878.6 119.0 %copy-start.59 = (f32[1024]{0:T(1024)S(1)}, f32[1024]{0:T(1024)}, u32[]{:S(2)}) copy-start(f32[1024]{0:T(1024)} %param.21) | copy-start | bytes 12292
  887.2 116.8 %copy-start.39 = (f32[4,512]{1,0:T(4,128)S(1)}, f32[4,512]{1,0:T(4,128)}, u32[]{:S(2)}) copy-start(f32[4,512]{1,0:T(4,128)} %copy-done.38) | copy-start | bytes 24580
  887.2 116.8 %copy-start.43 = (f32[4,512]{1,0:T(4,128)S(1)}, f32[4,512]{1,0:T(4,128)}, u32[]{:S(2)}) copy-start(f32[4,512]{1,0:T(4,128)} %copy-done.42) | copy-start | bytes 24580
  887.2 116.8 %copy-start.49 = (f32[4,512]{1,0:T(4,128)S(1)}, f32[4,512]{1,0:T(4,128)}, u32[]{:S(2)}) copy-start(f32[4,512]{1,0:T(4,128)} %copy-done.48) | copy-start | bytes 24580
  887.2 116.8 %copy-start.51 = (f32[4,512]{1,0:T(4,128)S(1)}, f32[4,512]{1,0:T(4,128)}, u32[]{:S(2)}) copy-start(f32[4,512]{1,0:T(4,128)} %copy-done.50) | copy-start | bytes 24580
  1004.6 182.3 %copy-start.1 = (bf16[8,4,1024,16]{2,3,1,0:T(8,128)(2,1)S(1)}, bf16[8,4,1024,16]{2,3,1,0:T(8,128)(2,1)}, u32[]{:S(2)}) copy-start(bf16[8,4,1024,16]{2,3,1,0:T(8,128)(2,1)} %param.30) | copy-start | bytes 3145732
  (58 other events, 910.0 us)
Sparse Core Ops, SparseCore 0:
  10.7 44.4 all-gather.7
  64.2 41.3 all-gather.15
  107.7 32.5 all-gather.13
  142.3 47.3 all-gather.11
  192.5 155.1 all-reduce.10
  349.7 47.6 all-gather.9
  428.0 155.0 all-reduce.12
  623.6 54.6 reduce-scatter.4
  691.6 54.6 reduce-scatter.2
  749.2 86.4 all-reduce.18
  838.2 159.3 all-reduce.14
  1002.2 170.0 all-reduce.16
where the time goes:
time: 1200 us; the launch traced here: 1190 us
  waiting for transfers between devices  725 us (60%)
  matrix products  235 us (20%)
  other arithmetic  94.6 us (8%)
  blocking collectives  82.8 us (7%)
  local copies, waits for them, and re-layouts  39.2 us (3%)
  between operations  15.4 us (1%)
    psum x1, waiting for transfers between devices, per_device(): lax.psum((down_total, qkv_up_total, fc1_up_total, proj_down_total, fc2_do...  155 us
    psum x1, waiting for transfers between devices, per_device(): lax.psum((normed_two_part, fc1_rank_part), 'tensor')  134 us
    psum x1, waiting for transfers between devices, per_device(): lax.psum((proj_part, proj_rank_part), 'tensor')  129 us
    psum x1, waiting for transfers between devices, per_device(): grad_normed, grad_rank_total = lax.psum((normed_part, rank_part), 'tensor')  110 us
    psum x1, waiting for transfers between devices, per_device(): lax.psum(mlp_part.astype(jnp.bfloat16), 'tensor').astype(jnp.float32)  72.2 us
    all_gather x1, waiting for transfers between devices, per_device(): lax.all_gather(w_qkv, ('shard', 'context'), axis=0, tiled=True)  37.4 us
    all_gather x1, waiting for transfers between devices, per_device(): lax.all_gather(w_fc1, ('shard', 'context'), axis=0, tiled=True)  36.6 us
    convert_element_type x1, other arithmetic, per_device(): grad_scores = (probs_again * (grad_probs - row_inner)).astype(jnp.bfloat16)  28.5 us
  transfers between devices with their start and end apart: 12, of which 11 were waited for; matrix products, arithmetic and copies ran while one was open for 22% of the time, Pallas kernels for 0%

commit v1 on v0

v1 whole, which is shorter than its diff:
```python
import functools
import math

import jax
import jax.numpy as jnp
from jax import lax
from jax.experimental import pallas as pl
from jax.experimental.pallas import tpu as pltpu
from jax.sharding import PartitionSpec as P

HEAD_DIM = 64
PAIR = 2 * HEAD_DIM
EPS = 1e-06
LOG2E = math.log2(math.e)
SCORE = 1.0 / math.sqrt(HEAD_DIM)
F32 = jnp.float32
BF16 = jnp.bfloat16
NT = (((1,), (1,)), ((), ()))
TN = (((0,), (0,)), ((), ()))


def dot(a, b):
    return jnp.dot(a, b, preferred_element_type=F32)


def dot_nt(a, b):
    return lax.dot_general(a, b, NT, preferred_element_type=F32)


def dot_tn(a, b):
    return lax.dot_general(a, b, TN, preferred_element_type=F32)


def head_masks(rows):
    lane = lax.broadcasted_iota(jnp.int32, (rows, PAIR), 1)
    return lane < HEAD_DIM


def attend_kernel(block, x_ref, o_ref, lse_ref):
    rows = x_ref.shape[0]
    keys = x_ref[:, PAIR : 2 * PAIR]
    values = jnp.concatenate(
        [x_ref[:, 2 * PAIR : 3 * PAIR], jnp.ones((rows, PAIR), BF16)], axis=1
    )
    first = head_masks(block)

    def step(i, carry):
        at = pl.ds(pl.multiple_of(i * block, block), block)
        q = x_ref[at, :PAIR]
        outs = []
        logs = []
        for head in range(2):
            mine = first if head == 0 else jnp.logical_not(first)
            s = dot_nt(jnp.where(mine, q, jnp.zeros_like(q)), keys)
            peak = jnp.max(s, axis=1, keepdims=True)
            e = jnp.exp2((s - peak) * (SCORE * LOG2E))
            acc = dot(e.astype(BF16), values)
            total = acc[:, PAIR:]
            outs.append(acc[:, :PAIR] / total)
            logs.append(peak * (SCORE * LOG2E) + jnp.log2(total))
        o_ref[at, :] = jnp.where(first, outs[0], outs[1]).astype(BF16)
        lane = lax.broadcasted_iota(jnp.int32, (block, PAIR), 1)
        both = jnp.where(lane == 0, logs[0], logs[1])
        lse_ref[0, :, at] = jnp.transpose(both)[:8]
        return carry

    lax.fori_loop(0, rows // block, step, 0)


def attend(qkv):
    rows, width = qkv.shape
    pairs = width // (3 * PAIR)
    block = min(256, rows)
    return pl.pallas_call(
        functools.partial(attend_kernel, block),
        grid=(pairs,),
        in_specs=[pl.BlockSpec((rows, 3 * PAIR), lambda p: (0, p))],
        out_specs=[
            pl.BlockSpec((rows, PAIR), lambda p: (0, p)),
            pl.BlockSpec((1, 8, rows), lambda p: (p, 0, 0)),
        ],
        out_shape=[
            jax.ShapeDtypeStruct((rows, pairs * PAIR), BF16),
            jax.ShapeDtypeStruct((pairs, 8, rows), F32),
        ],
        cost_estimate=pl.CostEstimate(
            flops=pairs * 2 * rows * rows * 256 * 4,
            bytes_accessed=rows * pairs * PAIR * 8,
            transcendentals=pairs * 2 * rows * rows,
        ),
        name="attend",
    )(qkv)


def attend_back_kernel(block, x_ref, go_ref, o_ref, lse_ref, g_ref, gq_ref, d_ref):
    rows = x_ref.shape[0]
    first = head_masks(block)
    prod = o_ref[...].astype(F32) * go_ref[...].astype(F32)
    lane8 = lax.broadcasted_iota(jnp.int32, (8, PAIR), 1) // HEAD_DIM
    row8 = lax.broadcasted_iota(jnp.int32, (8, PAIR), 0)
    d_ref[...] = lax.dot_general(
        (lane8 == row8).astype(F32),
        prod,
        NT,
        preferred_element_type=F32,
        precision=lax.Precision.HIGHEST,
    )
    gq_ref[...] = jnp.zeros_like(gq_ref)

    def step(i, carry):
        at = pl.ds(pl.multiple_of(i * block, block), block)
        k = x_ref[at, PAIR : 2 * PAIR]
        v = x_ref[at, 2 * PAIR : 3 * PAIR]
        q = x_ref[:, :PAIR]
        go = go_ref[...]
        gks = []
        gvs = []
        gq = None
        for head in range(2):
            mine = first if head == 0 else jnp.logical_not(first)
            k_own = jnp.where(mine, k, jnp.zeros_like(k))
            v_own = jnp.where(mine, v, jnp.zeros_like(v))
            s = dot_nt(k_own, q)
            gp = dot_nt(v_own, go)
            p = jnp.exp2(s * (SCORE * LOG2E) - lse_ref[0, head : head + 1, :])
            gs = (p * (gp - d_ref[head : head + 1, :])).astype(BF16)
            gks.append(dot(gs, q))
            gvs.append(dot(p.astype(BF16), go))
            part = dot(jnp.transpose(k_own), gs)
            gq = part if gq is None else gq + part
        gq_ref[...] += gq
        g_ref[at, PAIR : 2 * PAIR] = (jnp.where(first, gks[0], gks[1]) * SCORE).astype(BF16)
        g_ref[at, 2 * PAIR : 3 * PAIR] = jnp.where(first, gvs[0], gvs[1]).astype(BF16)
        return carry

    lax.fori_loop(0, rows // block, step, 0)
    g_ref[:, :PAIR] = (jnp.transpose(gq_ref[...]) * SCORE).astype(BF16)


def attend_back(qkv, go, o, lse):
    rows, width = qkv.shape
    pairs = width // (3 * PAIR)
    block = min(256, rows)
    return pl.pallas_call(
        functools.partial(attend_back_kernel, block),
        grid=(pairs,),
        in_specs=[
            pl.BlockSpec((rows, 3 * PAIR), lambda p: (0, p)),
            pl.BlockSpec((rows, PAIR), lambda p: (0, p)),
            pl.BlockSpec((rows, PAIR), lambda p: (0, p)),
            pl.BlockSpec((1, 8, rows), lambda p: (p, 0, 0)),
        ],
        out_specs=pl.BlockSpec((rows, 3 * PAIR), lambda p: (0, p)),
        out_shape=jax.ShapeDtypeStruct((rows, width), BF16),
        scratch_shapes=[pltpu.VMEM((PAIR, rows), F32), pltpu.VMEM((8, rows), F32)],
        cost_estimate=pl.CostEstimate(
            flops=pairs * 2 * rows * rows * 256 * 10,
            bytes_accessed=rows * pairs * PAIR * 16,
            transcendentals=pairs * 2 * rows * rows,
        ),
        name="attend_back",
    )(qkv, go, o, lse)


def mlp_kernel(
    block,
    n_ref,
    gb_ref,
    f_ref,
    gm_ref,
    ft_ref,
    gmt_ref,
    w1_ref,
    w2_ref,
    u1_ref,
    d2_ref,
    branch_ref,
    gn_ref,
    m_ref,
    gf_ref,
    gf1_ref,
    gf2_ref,
):
    rows = n_ref.shape[0]

    @pl.when(pl.program_id(0) == 0)
    def _():
        branch_ref[...] = jnp.zeros_like(branch_ref)
        gn_ref[...] = jnp.zeros_like(gn_ref)
        m_ref[...] = jnp.zeros_like(m_ref)
        gf_ref[...] = jnp.zeros_like(gf_ref)

    gf1_ref[...] = jnp.zeros_like(gf1_ref)
    gf2_ref[...] = jnp.zeros_like(gf2_ref)

    def step(i, carry):
        at = pl.ds(pl.multiple_of(i * block, block), block)
        w1 = w1_ref[...]
        w2 = w2_ref[...]
        u1 = u1_ref[...]
        d2 = d2_ref[...]
        z = dot(n_ref[at, :], w1) + dot(f_ref[at, :], u1)
        cdf = 0.5 * (1.0 + lax.erf(z * (1.0 / math.sqrt(2.0))))
        a = (z * cdf).astype(BF16)
        slope = cdf + z * (jnp.exp2(z * z * (-0.5 * LOG2E)) * (1.0 / math.sqrt(2.0 * math.pi)))
        ga = dot(gb_ref[at, :], w2) + dot(gm_ref[at, :], d2)
        gz = (ga * slope).astype(BF16)
        branch_ref[at, :] += dot_nt(a, w2)
        m_ref[at, :] += dot_nt(a, d2)
        gn_ref[at, :] += dot_nt(gz, w1)
        gf_ref[at, :] += dot_nt(gz, u1)
        gf1_ref[...] += dot(ft_ref[:, at], gz)
        gf2_ref[...] += dot(gmt_ref[:, at], a)
        return carry

    lax.fori_loop(0, rows // block, step, 0)


def mlp(n, gb, f, gm, w1, w2, u1, d2):
    rows, model = n.shape
    hidden = w1.shape[1]
    rank = f.shape[1]
    chunk = min(512, hidden)
    block = min(256, rows)
    whole = lambda shape: pl.BlockSpec(shape, lambda j: (0, 0))
    part = lambda depth: pl.BlockSpec((depth, chunk), lambda j: (0, j))
    return pl.pallas_call(
        functools.partial(mlp_kernel, block),
        grid=(hidden // chunk,),
        in_specs=[
            whole((rows, model)),
            whole((rows, model)),
            whole((rows, rank)),
            whole((rows, rank)),
            whole((rank, rows)),
            whole((rank, rows)),
            part(model),
            part(model),
            part(rank),
            part(rank),
        ],
        out_specs=[
            whole((rows, model)),
            whole((rows, model)),
            whole((rows, rank)),
            whole((rows, rank)),
            part(rank),
            part(rank),
        ],
        out_shape=[
            jax.ShapeDtypeStruct((rows, model), F32),
            jax.ShapeDtypeStruct((rows, model), F32),
            jax.ShapeDtypeStruct((rows, rank), F32),
            jax.ShapeDtypeStruct((rows, rank), F32),
            jax.ShapeDtypeStruct((rank, hidden), F32),
            jax.ShapeDtypeStruct((rank, hidden), F32),
        ],
        cost_estimate=pl.CostEstimate(
            flops=12 * rows * model * hidden,
            bytes_accessed=4 * model * hidden + 12 * rows * model,
            transcendentals=2 * rows * hidden,
        ),
        name="mlp",
    )(n, gb, f, gm, f.T, gm.T, w1, w2, u1, d2)


def normalize(values, gain, shift):
    centre = values - jnp.mean(values, axis=-1, keepdims=True)
    inverse = lax.rsqrt(jnp.mean(centre * centre, axis=-1, keepdims=True) + EPS)
    unit = centre * inverse
    return unit * gain + shift, unit, inverse


def norm_back(grad, unit, inverse, gain):
    scaled = grad * gain
    centred = scaled - jnp.mean(scaled, axis=-1, keepdims=True)
    return inverse * (centred - unit * jnp.mean(scaled * unit, axis=-1, keepdims=True))


def per_device(
    sizes,
    tokens,
    cotangent,
    adapter_index,
    ln1_gain,
    ln1_bias,
    ln2_gain,
    ln2_bias,
    layer_scale,
    w_qkv,
    w_proj,
    w_fc1,
    w_fc2,
    down_in,
    qkv_up,
    fc1_up,
    proj_down,
    fc2_down,
    out_up,
):
    shards, contexts, tensors = sizes
    half = contexts // 2
    sides = tensors // 2
    images, rows, model = tokens.shape
    rank = down_in.shape[-1]
    depth = w_fc1.shape[0]
    width = w_proj.shape[1]
    hidden = w_fc1.shape[1]
    pairs = width // PAIR
    adapters = down_in.shape[0]
    shard = lax.axis_index("shard")
    context = lax.axis_index("context")
    tensor = lax.axis_index("tensor")
    side, core = tensor // 2, tensor % 2
    high = context // half

    ring = {
        "shard": [(i, (i + 1) % shards) for i in range(shards)],
        "context": [(i, (i + 1) % contexts) for i in range(contexts)],
        "tensor": [(i, (i + 2) % tensors) for i in range(tensors)],
    }
    count = {"shard": shards, "context": contexts, "tensor": sides}
    twin = [(i, i ^ 1) for i in range(tensors)]

    def hop(value, axis):
        return lax.ppermute(value, axis, ring[axis])

    def swap(value):
        return lax.ppermute(value, "tensor", twin)

    def around(value, axis):
        out = [value]
        for _ in range(count[axis] - 1):
            out.append(hop(out[-1], axis))
        return out

    to_owner = []
    to_home = []
    to_home_far = {far: [] for far in range(sides)}
    for c in range(contexts):
        for s in range(sides):
            for k in range(2):
                here = c * tensors + 2 * s + k
                source = 2 * (c % half) + k
                to_owner.append((source * tensors + 2 * s + c // half, here))
                for far in range(sides):
                    there = (s + far) % sides
                    to_home_far[far].append((here, source * tensors + 2 * there + c // half))
    plane = ("context", "tensor")

    def block_of(array, index):
        return lax.dynamic_index_in_dim(array, index, 0, keepdims=False)

    x_own = lax.ppermute(block_of(tokens, tensor), plane, to_owner)
    gy_own = lax.ppermute(block_of(cotangent, tensor), plane, to_owner)

    attn_own = jnp.concatenate(
        [w_qkv[:, j, p * PAIR : (p + 1) * PAIR] for p in range(pairs) for j in range(3)] + [w_proj],
        axis=1,
    )

    def gather_mid(value, first, last):
        parts = jnp.concatenate(around(value, first), axis=0)
        out = {}
        for i, item in enumerate(around(parts, "shard")):
            for j, got in enumerate(around(item, last)):
                for k in range(count[first]):
                    piece = got[k * depth : (k + 1) * depth]
                    far, near = (k, j) if first == "tensor" else (j, k)
                    out[(i, near, far)] = piece
        return out

    def gather_flat(value):
        line = around(value, "shard")
        out = {}
        middle = max(shards // 2, 1)
        for start, stop, first, last in (
            (0, middle, "tensor", "context"),
            (middle, shards, "context", "tensor"),
        ):
            if start == stop:
                continue
            parts = jnp.concatenate(line[start:stop], axis=0)
            for a, item in enumerate(around(parts, first)):
                for b, got in enumerate(around(item, last)):
                    far, near = (a, b) if first == "tensor" else (b, a)
                    for i in range(start, stop):
                        k = i - start
                        out[(i, near, far)] = got[k * depth : (k + 1) * depth]
        return out

    def gather_plain(value):
        whole = lax.all_gather(value, ("shard", "context"), axis=0, tiled=True)
        return around(whole, "tensor")

    ringed = shards * contexts * sides <= 16

    def stack(parts):
        return [
            jnp.concatenate(
                [parts[(i, j, far)] for i in range(shards) for j in range(contexts)], axis=0
            )
            for far in range(sides)
        ]

    if ringed:
        attn_parts = stack(gather_flat(attn_own))
        fc1_parts = stack(gather_mid(w_fc1, "tensor", "context"))
        fc2_parts = stack(gather_mid(w_fc2, "context", "tensor"))
        order = [
            ((shard - i) % shards) * contexts + (context - j) % contexts
            for i in range(shards)
            for j in range(contexts)
        ]
        back = [
            ((shard - b // contexts) % shards) * contexts + (context - b % contexts) % contexts
            for b in range(shards * contexts)
        ]
    else:
        attn_parts = gather_plain(attn_own)
        fc1_parts = gather_plain(w_fc1)
        fc2_parts = gather_plain(w_fc2)
        order = back = None

    def reorder(array, blocks):
        if blocks is None:
            return array
        axis = array.ndim - 1
        return jnp.concatenate(
            [lax.dynamic_slice_in_dim(array, b * depth, depth, axis) for b in blocks], axis=axis
        )

    shuffle = lambda array: reorder(array, order)
    restore = lambda array: reorder(array, back)

    def adapter_of(far):
        return block_of(adapter_index, 2 * ((side + far) % sides) + high)

    def up_pack(index):
        up = block_of(qkv_up, index)
        return jnp.concatenate(
            [up[0], up[1], up[2], block_of(fc1_up, index)]
            + [block_of(proj_down, index).T, block_of(fc2_down, index).T],
            axis=1,
        )

    packs = [up_pack(adapter_of(0))]
    for far in range(1, sides):
        send = [(i, (i + 2 * far) % tensors) for i in range(tensors)]
        packs.append(lax.ppermute(up_pack(adapter_of(far)), "tensor", send))
    mine = adapter_of(0)
    down = block_of(down_in, mine)
    down_t = shuffle(jnp.transpose(down, (0, 2, 1)).reshape(4 * rank, model))
    out_t = shuffle(block_of(out_up, mine))

    zero = jnp.zeros((rank, PAIR), BF16)

    def spread(pack):
        lines = []
        for j in range(3):
            cells = []
            for p in range(pairs):
                start = j * width + p * PAIR
                for k in range(3):
                    cells.append(pack[:, start : start + PAIR] if k == j else zero)
            lines.append(jnp.concatenate(cells, axis=1))
        return jnp.concatenate(lines, axis=0)

    qkv_lift = jnp.concatenate([spread(pack) for pack in packs], axis=1)
    base = 3 * width
    fc1_lift = jnp.concatenate([pack[:, base : base + hidden] for pack in packs], axis=1)
    base += hidden
    proj_t = jnp.concatenate([pack[:, base : base + width] for pack in packs], axis=1)
    base += width
    fc2_t = jnp.concatenate([pack[:, base : base + hidden] for pack in packs], axis=1)

    gain_one, bias_one = shuffle(ln1_gain), shuffle(ln1_bias)
    gain_two, bias_two = shuffle(ln2_gain), shuffle(ln2_bias)
    scale = shuffle(layer_scale)

    x_own = shuffle(x_own)
    x_all = jnp.concatenate([x_own, swap(x_own)], axis=0).astype(F32)
    normed, unit_one, inverse_one = normalize(x_all, gain_one, bias_one)
    n1 = normed.astype(BF16)
    u = dot_nt(n1, down_t[: 3 * rank]).astype(BF16)
    w_in = jnp.concatenate([part[:, : 3 * width] for part in attn_parts], axis=1)
    w_out = jnp.concatenate([part[:, 3 * width :] for part in attn_parts], axis=1)
    qkv = (dot(n1, w_in) + dot(u, qkv_lift)).astype(BF16)

    groups = [[h * half + i for i in range(half)] for h in range(2)]

    def to_heads(array, cell):
        if half == 1:
            return array
        cells = array.reshape(array.shape[0], -1, cell)
        moved = lax.all_to_all(
            cells, "context", 1, 0, axis_index_groups=groups, tiled=True
        )
        return moved.reshape(moved.shape[0], -1)

    def to_rows(array, cell):
        if half == 1:
            return array
        cells = array.reshape(array.shape[0], -1, cell)
        moved = lax.all_to_all(
            cells, "context", 0, 1, axis_index_groups=groups, tiled=True
        )
        return moved.reshape(moved.shape[0], -1)

    qkv_heads = to_heads(qkv, 3 * PAIR)
    o_heads, lse = attend(qkv_heads)
    o = to_rows(o_heads, PAIR)
    attn_part = dot_nt(o, w_out)
    c_part = dot_nt(o, proj_t)
    c_own = (c_part[:rows] + swap(c_part[rows:])).astype(BF16)
    attn_out = attn_part[:rows] + swap(attn_part[rows:]) + dot(c_own, out_t[0])
    h = x_all[:rows] + scale[0] * attn_out
    normed, unit_two, inverse_two = normalize(h, gain_two, bias_two)
    n2_own = normed.astype(BF16)
    n2 = jnp.concatenate([n2_own, swap(n2_own)], axis=0)
    f = dot_nt(n2, down_t[3 * rank :]).astype(BF16)

    gy_own = shuffle(gy_own)
    gy_all = jnp.concatenate([gy_own, swap(gy_own)], axis=0)
    gb = (gy_all.astype(F32) * scale[1]).astype(BF16)
    gm = dot_nt(gb, out_t[1]).astype(BF16)

    branch_part, gn2_part, m_part, gf_part, g_fc1, g_fc2 = mlp(
        n2,
        gb,
        f,
        gm,
        jnp.concatenate(fc1_parts, axis=1),
        jnp.concatenate(fc2_parts, axis=1),
        fc1_lift,
        fc2_t,
    )
    m_own = (m_part[:rows] + swap(m_part[rows:])).astype(BF16)
    branch_far = swap(branch_part[rows:].astype(BF16)).astype(F32)
    branch = branch_part[:rows] + branch_far + dot(m_own, out_t[1])
    result_own = (h + scale[1] * branch).astype(BF16)
    g_out1 = dot_tn(m_own, gb[:rows])

    gf_own = (gf_part[:rows] + swap(gf_part[rows:])).astype(BF16)
    gn2 = gn2_part[:rows] + swap(gn2_part[rows:]) + dot(gf_own, down_t[3 * rank :])
    g_down3 = dot_tn(gf_own, n2_own)
    gh = gy_own.astype(F32) + norm_back(gn2, unit_two, inverse_two, gain_two)
    gattn_own = (scale[0] * gh).astype(BF16)
    gattn = jnp.concatenate([gattn_own, swap(gattn_own)], axis=0)
    gc = dot_nt(gattn, out_t[0]).astype(BF16)
    g_out0 = dot_tn(c_own, gattn_own)
    go = (dot(gattn, w_out) + dot(gc, proj_t)).astype(BF16)
    g_proj = dot_tn(gc, o)
    g = to_rows(attend_back(qkv_heads, to_heads(go, PAIR), o_heads, lse), 3 * PAIR)

    gu_part = dot_nt(g, qkv_lift)
    gu_own = (gu_part[:rows] + swap(gu_part[rows:])).astype(BF16)
    gn1_part = dot_nt(g, w_in)
    gn1 = gn1_part[:rows] + swap(gn1_part[rows:]) + dot(gu_own, down_t[: 3 * rank])
    g_up = dot_tn(u, g)
    g_down = dot_tn(gu_own, n1[:rows])
    input_own = gh + norm_back(gn1, unit_one[:rows], inverse_one[:rows], gain_one)

    def send_home(block):
        near = []
        for far in range(sides):
            got = lax.ppermute(block, plane, to_home_far[far])
            near += [got, swap(got)]
        return near

    def place(near, kind):
        out = jnp.zeros((images, rows, model), kind)
        for far in range(sides):
            for flip in range(2):
                where = 2 * ((side - far) % sides) + (core ^ flip)
                piece = near[2 * far + flip].astype(kind)[None]
                out = lax.dynamic_update_slice(out, piece, (where, 0, 0))
        return out

    result = place(send_home(restore(result_own)), BF16)
    input_grad = place(send_home(restore(input_own.astype(BF16))), F32)

    def slice_grads(far):
        cells = []
        for j in range(3):
            for p in range(pairs):
                start = ((far * pairs + p) * 3 + j) * PAIR
                cells.append(g_up[j * rank : (j + 1) * rank, start : start + PAIR])
        cells.append(g_fc1[:, far * hidden : (far + 1) * hidden])
        cells.append(g_proj[:, far * width : (far + 1) * width])
        cells.append(g_fc2[:, far * hidden : (far + 1) * hidden])
        return jnp.concatenate(cells, axis=1)

    shared = jnp.concatenate(
        [g_down.reshape(3, rank, model), g_down3[None], g_out0[None], g_out1[None]], axis=0
    )
    shared = restore(shared)
    both = shared + swap(shared)
    cut = model // 2
    own_half = lax.dynamic_slice_in_dim(both, core * cut, cut, 2)
    own_half = jnp.concatenate([own_half[j] for j in range(6)], axis=1)

    owners = jnp.stack([adapter_of(0)])
    gathered = [jnp.concatenate([slice_grads(0), own_half], axis=1).astype(BF16)]
    marks = [adapter_of(0)]
    for far in range(1, sides):
        send = [(i, (i - 2 * far) % tensors) for i in range(tensors)]
        pack = jnp.concatenate([slice_grads(far), own_half], axis=1).astype(BF16)
        gathered.append(lax.ppermute(pack, "tensor", send))
        marks.append(adapter_of(far))
    block = jnp.stack(gathered)
    mark = jnp.stack(marks)
    lane = jnp.arange(adapters, dtype=jnp.int32)
    pick = (mark[:, None] == lane[None, :]).astype(F32)
    if half > 1:
        steps = [[h * half + i for i in range(half)] for h in range(2)]
        block = lax.psum(block.astype(F32), "context", axis_index_groups=steps).astype(BF16)
        across = [(i, (i + half) % contexts) for i in range(contexts)]
    else:
        across = ring["context"]
    block = jnp.concatenate([block, lax.ppermute(block, "context", across)], axis=0)
    pick = jnp.concatenate([pick, lax.ppermute(pick, "context", across)], axis=0)
    blocks = around(block, "shard")
    picks = around(pick, "shard")
    all_blocks = jnp.concatenate(blocks, axis=0)
    all_picks = jnp.concatenate(picks, axis=0).astype(BF16)
    flat = all_blocks.reshape(all_blocks.shape[0], -1)
    totals = lax.dot_general(all_picks, flat, TN, preferred_element_type=F32)
    totals = totals.reshape(adapters, rank, -1)

    base = 3 * width
    qkv_grad = totals[:, :, :base].reshape(adapters, rank, 3, width)
    qkv_grad = jnp.transpose(qkv_grad, (0, 2, 1, 3))
    fc1_grad = totals[:, :, base : base + hidden]
    base += hidden
    proj_grad = jnp.transpose(totals[:, :, base : base + width], (0, 2, 1))
    base += width
    fc2_grad = jnp.transpose(totals[:, :, base : base + hidden], (0, 2, 1))
    base += hidden
    halves = totals[:, :, base:].reshape(adapters, rank, 6, cut)
    other = swap(halves)
    low = jnp.where(core == 0, halves, other)
    top = jnp.where(core == 0, other, halves)
    shared = jnp.transpose(jnp.concatenate([low, top], axis=3), (0, 2, 1, 3))
    down_grad = jnp.transpose(shared[:, :4], (0, 1, 3, 2))
    out_grad = shared[:, 4:]
    return (
        result,
        input_grad,
        down_grad,
        qkv_grad,
        fc1_grad,
        proj_grad,
        fc2_grad,
        out_grad,
    )


def solution(mesh):
    sizes = (mesh.shape["shard"], mesh.shape["context"], mesh.shape["tensor"])
    placed = (
        P("shard", "context", None),
        P("shard", "context", None),
        P("shard"),
        P(),
        P(),
        P(),
        P(),
        P(),
        P(("shard", "context"), None, "tensor"),
        P(("shard", "context"), "tensor"),
        P(("shard", "context"), "tensor"),
        P(("shard", "context"), "tensor"),
        P(),
        P(None, None, None, "tensor"),
        P(None, None, "tensor"),
        P(None, "tensor", None),
        P(None, "tensor", None),
        P(),
    )
    return jax.shard_map(
        functools.partial(per_device, sizes),
        mesh=mesh,
        in_specs=placed,
        out_specs=(
            P("shard", "context", None),
            P("shard", "context", None),
            P(),
            P(None, None, None, "tensor"),
            P(None, None, "tensor"),
            P(None, "tensor", None),
            P(None, "tensor", None),
            P(),
        ),
        check_vma=False,
    )
```

time: 1200 us -> 492 us (0.41)
  waiting for transfers between devices: 725 us -> 133 us
  matrix products: 235 us -> 34.5 us
  blocking collectives: 82.8 us -> 0 us
  Pallas kernels: 0 us -> 81.9 us
  local copies, waits for them, and re-layouts: 39.2 us -> 118 us
  starting transfers between devices: 1.95 us -> 62.6 us
  other arithmetic: 94.6 us -> 44.8 us
    psum x5 -> x0, waiting for transfers between devices: 601 us -> none  [the longest x1 155 us: per_device(): lax.psum((down_total, qkv_up_total, fc1_up_total, proj_down_total, fc2_do...]
    dot_general x50 -> x23, matrix products: 235 us -> 34.5 us  [the longest x8 13 us: dot(): return jnp.dot(a, b, preferred_element_type=F32)]
    ppermute x0 -> x59, waiting for transfers between devices: none -> 133 us  [the longest x31 95.5 us: hop(): return lax.ppermute(value, axis, ring[axis])]
    all_gather x5 -> x0, waiting for transfers between devices: 116 us -> none  [the longest x1 37.4 us: per_device(): lax.all_gather(w_qkv, ('shard', 'context'), axis=0, tiled=True)]
    pallas_call x0 -> x3, Pallas kernels: none -> 81.9 us  [the longest x1 33.2 us: mlp(): pl.pallas_call(functools.partial(mlp_kernel, block), grid=(hidden // chun...]
    ppermute x0 -> x59, starting transfers between devices: none -> 62.6 us  [the longest x31 25.4 us: hop(): return lax.ppermute(value, axis, ring[axis])]
    psum x3 -> x0, blocking collectives: 56.6 us -> none  [the longest x1 21.9 us: per_device(): grad_normed, grad_rank_total = lax.psum((normed_part, rank_part), 'tensor')]
    convert_element_type x4 -> x10, other arithmetic: 58.5 us -> 8.03 us  [the longest x1 2.77 us: per_device(): gattn_own = (scale[0] * gh).astype(BF16)]
  transfers between devices with their start and end apart: 12 -> 59, of which waited for: 11 -> 22; matrix products, arithmetic and copies ran while one was open for 22% -> 33% of each run, Pallas kernels for 0% -> 4%
where the time goes in v1:
time: 492 us; the launch traced here: 482 us
  waiting for transfers between devices  133 us (27%)
  local copies, waits for them, and re-layouts  118 us (24%)
  Pallas kernels  81.9 us (17%)
  starting transfers between devices  62.6 us (13%)
  other arithmetic  44.8 us (9%)
  matrix products  34.5 us (7%)
  between operations  7.46 us (2%)
    ppermute x31, waiting for transfers between devices, hop(): return lax.ppermute(value, axis, ring[axis])  95.5 us
    unnamed x346, local copies, waits for them, and re-layouts  69.5 us
    pallas_call x1, Pallas kernels, mlp(): pl.pallas_call(functools.partial(mlp_kernel, block), grid=(hidden // chun...  33.2 us
    pallas_call x1, Pallas kernels, attend_back(): pl.pallas_call(functools.partial(attend_back_kernel, block), grid=(pairs,...  28.2 us
    ppermute x31, starting transfers between devices, hop(): return lax.ppermute(value, axis, ring[axis])  25.4 us
    pallas_call x1, Pallas kernels, attend(): pl.pallas_call(functools.partial(attend_kernel, block), grid=(pairs,), in...  20.5 us
    ppermute x18, starting transfers between devices, swap(): return lax.ppermute(value, 'tensor', twin)  16.6 us
    ppermute x1, waiting for transfers between devices, per_device(): lax.ppermute(pick, 'context', across)  15.8 us
  transfers between devices with their start and end apart: 59, of which 22 were waited for; matrix products, arithmetic and copies ran while one was open for 33% of the time, Pallas kernels for 4%

profile of v1, /device:TPU:1, one launch (start us, length us, event | category | flops | bytes accessed | tf_op | source)
XLA Modules:
  0.0 482.3 jit_solution(7457268563601962699)
XLA Ops:
  27.0 6.7 %collective-permute-start.25 = (bf16[128,1024]{1,0:T(8,128)(2,1)}, bf16[128,1024]{1,0:T(8,128)(2,1)}, u32[]{:S(2)}, u32[]{:S(2)}) collective-permute-start(bf16[128,1024]{1,0:T(8,128)(2,1)} %param.29), channel_id=1, source_target_pairs={{0,4},{4,0},{1,5},{5,1},{2,6},{6,2},{3,7},{7,3},{8,12},{12,8},{9,1... | collective-permute-start | bytes 786440 | tf_op jit(solution)/shard_map/ppermute | solution.py:326
  60.2 4.1 collective-permute-start.15
  72.0 11.8 %collective-permute-done.26 = bf16[256,1024]{1,0:T(8,128)(2,1)} collective-permute-done((bf16[256,1024]{1,0:T(8,128)(2,1)}, bf16[256,1024]{1,0:T(8,128)(2,1)}, u32[]{:S(2)}, u32[]{:S(2)}) %collective-permute-start.26) | collective-permute-done | bytes 524320 | tf_op jit(solution)/shard_map/ppermute | solution.py:326
  89.8 5.7 %collective-permute-done.18 = bf16[256,1024]{1,0:T(8,128)(2,1)S(1)} collective-permute-done((bf16[256,1024]{1,0:T(8,128)(2,1)S(1)}, bf16[256,1024]{1,0:T(8,128)(2,1)S(1)}, u32[]{:S(2)}, u32[]{:S(2)}) %collective-permute-start.18) | collective-permute-done | bytes 524320 | tf_op jit(solution)/shard_map/ppermute | solution.py:326
  95.5 7.9 %collective-permute-done.19 = bf16[256,1024]{1,0:T(8,128)(2,1)S(1)} collective-permute-done((bf16[256,1024]{1,0:T(8,128)(2,1)S(1)}, bf16[256,1024]{1,0:T(8,128)(2,1)S(1)}, u32[]{:S(2)}, u32[]{:S(2)}) %collective-permute-start.19) | collective-permute-done | bytes 524320 | tf_op jit(solution)/shard_map/ppermute | solution.py:326
  113.5 15.3 %collective-permute-done.8 = bf16[256,1024]{1,0:T(8,128)(2,1)S(1)} collective-permute-done((bf16[256,1024]{1,0:T(8,128)(2,1)S(1)}, bf16[256,1024]{1,0:T(8,128)(2,1)S(1)}, u32[]{:S(2)}, u32[]{:S(2)}) %collective-permute-start.8) | collective-permute-done | bytes 524320 | tf_op jit(solution)/shard_map/ppermute | solution.py:326
  136.5 5.5 %collective-permute-done.27 = bf16[256,1024]{1,0:T(8,128)(2,1)} collective-permute-done((bf16[256,1024]{1,0:T(8,128)(2,1)}, bf16[256,1024]{1,0:T(8,128)(2,1)}, u32[]{:S(2)}, u32[]{:S(2)}) %collective-permute-start.27) | collective-permute-done | bytes 524320 | tf_op jit(solution)/shard_map/ppermute | solution.py:326
  145.7 4.0 collective-permute-done.10
  163.8 20.5 %attend.1 = (bf16[1024,512]{1,0:T(8,128)(2,1)}, f32[4,8,1024]{2,1,0:T(8,128)}) custom-call(bf16[1024,1536]{1,0:T(8,128)(2,1)} %add_convert_fusion.x_ref), custom_call_target="tpu_custom_call" | custom-call | flops 8589934592 | bytes 4194304 | tf_op jit(solution)/shard_map/attend/pallas_call | solution.py:74
  212.1 8.0 %collective-permute-done.24 = bf16[256,1024]{1,0:T(8,128)(2,1)S(1)} collective-permute-done((bf16[256,1024]{1,0:T(8,128)(2,1)}, bf16[256,1024]{1,0:T(8,128)(2,1)S(1)}, u32[]{:S(2)}, u32[]{:S(2)}) %collective-permute-start.24) | collective-permute-done | bytes 524320 | tf_op jit(solution)/shard_map/ppermute | solution.py:326
  223.5 5.5 %collective-permute-done.32 = bf16[256,1024]{1,0:T(8,128)(2,1)S(1)} collective-permute-done((bf16[256,1024]{1,0:T(8,128)(2,1)}, bf16[256,1024]{1,0:T(8,128)(2,1)S(1)}, u32[]{:S(2)}, u32[]{:S(2)}) %collective-permute-start.32) | collective-permute-done | bytes 524320 | tf_op jit(solution)/shard_map/ppermute | solution.py:326
  229.1 7.8 %maximum_maximum_fusion.w2_ref = bf16[1024,2048]{1,0:T(8,128)(2,1)} fusion(bf16[256,1024]{1,0:T(8,128)(2,1)S(1)} %collective-permute-done.32, bf16[256,1024]{1,0:T(8,128)(2,1)} %collective-permute-done.31, bf16[256,1024]{1,0:T(8,128)(2,1)} %collective-permute-done.30, bf16[256,1024]{1,0:T(8,128)(2,1)} %collective-permute-done.29, ...), kind=kLoop, calls=%fused_computation.2 | loop fusion | flops 20971520 | bytes 8388608 | tf_op jit(solution)/shard_map/concatenate | solution.py:534
  242.8 33.2 %mlp.1 = (f32[1024,1024]{1,0:T(8,128)}, f32[1024,1024]{1,0:T(8,128)}, f32[1024,16]{1,0:T(8,128)}, f32[1024,16]{1,0:T(8,128)}, f32[16,2048]{1,0:T(8,128)}, /*index=5*/f32[16,2048]{1,0:T(8,128)}) custom-call(bf16[1024,1024]{1,0:T(8,128)(2,1)} %pad_maximum_fusion.3.n_ref, bf16[1024,1024]{1,0:T(8,128)(2,1)} %copy-done.4, bf16[1024,16]{1,0:T(8,128)(2,1)} %copy.41.f_ref, ...), custom_call_target="tpu_custom_call" | custom-call | flops 25769803776 | bytes 20971520 | tf_op jit(solution)/shard_map/mlp/pallas_call | solution.py:227
  303.4 28.2 %attend_back.1 = bf16[1024,1536]{1,0:T(8,128)(2,1)} custom-call(bf16[1024,1536]{1,0:T(8,128)(2,1)} %add_convert_fusion.x_ref, bf16[1024,512]{1,0:T(8,128)(2,1)} %add_convert_fusion.3.go_ref, bf16[1024,512]{1,0:T(8,128)(2,1)} %get-tuple-element.16.o_ref, f32[4,8,1024]{2,1,0:T(8,128)} %get-tuple-element.21.lse_ref), custom_call_target="tpu_custom_call" | custom-call | flops 21474836480 | bytes 8388608 | tf_op jit(solution)/shard_map/attend_back/pallas_call | solution.py:144
  347.9 6.2 %collective-permute-done.53 = bf16[16,6144]{1,0:T(8,128)(2,1)S(1)} collective-permute-done((bf16[16,6144]{1,0:T(8,128)(2,1)S(1)}, bf16[16,6144]{1,0:T(8,128)(2,1)S(1)}, u32[]{:S(2)}, u32[]{:S(2)}) %collective-permute-start.53) | collective-permute-done | bytes 196640 | tf_op jit(solution)/shard_map/ppermute | solution.py:609
  366.4 4.1 collective-permute-start.48
  370.5 15.8 %collective-permute-done.48 = bf16[2,8]{0,1:T(8,128)(2,1)S(1)} collective-permute-done((bf16[2,8]{0,1:T(8,128)(2,1)S(1)}, bf16[2,8]{0,1:T(8,128)(2,1)S(1)}, u32[]{:S(2)}, u32[]{:S(2)}) %collective-permute-start.48) | collective-permute-done | bytes 64 | tf_op jit(solution)/shard_map/ppermute | solution.py:622
  390.6 4.2 collective-permute-done.50
  394.8 4.2 collective-permute-done.51
  399.2 5.5 %collective-permute-start.36 = (bf16[512,1024]{1,0:T(8,128)(2,1)}, bf16[512,1024]{1,0:T(8,128)(2,1)S(1)}, u32[]{:S(2)}, u32[]{:S(2)}) collective-permute-start(bf16[512,1024]{1,0:T(8,128)(2,1)} %collective-permute-done.35), channel_id=1, source_target_pairs={{0,1},{1,0},{2,3},{3,2},{4,5},{5,4},{6,7},{7,6},{8,9},{9,8},{10,11... | collective-permute-start | bytes 3145736 | tf_op jit(solution)/shard_map/ppermute | solution.py:329
  416.9 9.0 %collective-permute-done.56 = bf16[4,16,6144]{2,1,0:T(8,128)(2,1)S(1)} collective-permute-done((bf16[4,16,6144]{2,1,0:T(8,128)(2,1)}, bf16[4,16,6144]{2,1,0:T(8,128)(2,1)S(1)}, u32[]{:S(2)}, u32[]{:S(2)}) %collective-permute-start.56) | collective-permute-done | bytes 786464 | tf_op jit(solution)/shard_map/ppermute | solution.py:326
  431.0 7.6 %collective-permute-done.44 = bf16[512,1024]{1,0:T(8,128)(2,1)} collective-permute-done((bf16[512,1024]{1,0:T(8,128)(2,1)S(1)}, bf16[512,1024]{1,0:T(8,128)(2,1)}, u32[]{:S(2)}, u32[]{:S(2)}) %collective-permute-start.44) | collective-permute-done | bytes 1048608 | tf_op jit(solution)/shard_map/ppermute | solution.py:567
  439.2 6.6 %collective-permute-done.57 = bf16[4,16,6144]{2,1,0:T(8,128)(2,1)S(1)} collective-permute-done((bf16[4,16,6144]{2,1,0:T(8,128)(2,1)S(1)}, bf16[4,16,6144]{2,1,0:T(8,128)(2,1)S(1)}, u32[]{:S(2)}, u32[]{:S(2)}) %collective-permute-start.57) | collective-permute-done | bytes 786464 | tf_op jit(solution)/shard_map/ppermute | solution.py:326
  446.4 11.9 %concatenate.266 = bf16[16,98304]{1,0:T(8,128)(2,1)} concatenate(bf16[1,98304]{1,0:T(2,128)(2,1)S(1)} %bitcast.265, bf16[1,98304]{1,0:T(2,128)(2,1)S(1)} %bitcast.266, bf16[2,98304]{1,0:T(2,128)(2,1)} %bitcast.267, bf16[4,98304]{1,0:T(4,128)(2,1)S(1)} %bitcast.258, bf16[4,98304]{1,0:T(4,128)(2,1)S(1)} %bitcast.259, bf16[4,98304]{1,0:T(4,128)(2,1)S(1)} %bitcast.260), dimensions={0} | concatenate | bytes 6291456 | tf_op jit(solution)/shard_map/concatenate | solution.py:625
  (584 shorter events, 235.5 us)
Async XLA Ops:
  0.7 59.6 %collective-permute-start.17 = (bf16[128,1024]{1,0:T(8,128)(2,1)}, bf16[128,1024]{1,0:T(8,128)(2,1)}, u32[]{:S(2)}, u32[]{:S(2)}) collective-permute-start(bf16[128,1024]{1,0:T(8,128)(2,1)} %param.28), channel_id=1, source_target_pairs={{0,2},{1,3},{2,0},{3,1},{4,6},{5,7},{6,4},{7,5},{8,10},{9,11},{10,... | collective-permute-start | bytes 786440 | tf_op jit(solution)/shard_map/ppermute | solution.py:326
  5.0 98.4 %collective-permute-start = (bf16[512,1024]{1,0:T(8,128)(2,1)}, bf16[512,1024]{1,0:T(8,128)(2,1)}, u32[]{:S(2)}, u32[]{:S(2)}) collective-permute-start(bf16[512,1024]{1,0:T(8,128)(2,1)} %dynamic-slice_bitcast_fusion.1), channel_id=1, source_target_pairs={{0,0},{4,1},{2,2},{6,3},{1,4},{5,5},{3,6},{7,7},{8,8},{12,9},{10,1... | collective-permute-start | bytes 3145736 | tf_op jit(solution)/shard_map/ppermute | solution.py:354
  19.8 33.9 %collective-permute-start.11 = (bf16[16,3072]{1,0:T(8,128)(2,1)}, bf16[16,3072]{1,0:T(8,128)(2,1)}, u32[]{:S(2)}, u32[]{:S(2)}) collective-permute-start(bf16[16,3072]{1,0:T(8,128)(2,1)} %constant_dynamic-update-slice_fusion.62), channel_id=1, source_target_pairs={{0,2},{1,3},{2,0},{3,1},{4,6},{5,7},{6,4},{7,5},{8,10},{9,11},{10,... | collective-permute-start | bytes 294920 | tf_op jit(solution)/shard_map/ppermute | solution.py:450
  25.7 30.7 %collective-permute-start.2 = (bf16[128,1024]{1,0:T(8,128)(2,1)}, bf16[128,1024]{1,0:T(8,128)(2,1)S(1)}, u32[]{:S(2)}, u32[]{:S(2)}) collective-permute-start(bf16[128,1024]{1,0:T(8,128)(2,1)} %get-tuple-element.100), channel_id=1, source_target_pairs={{0,8},{8,16},{16,24},{24,0},{1,9},{9,17},{17,25},{25,1},{2,10},{10... | collective-permute-start | bytes 786440 | tf_op jit(solution)/shard_map/ppermute | solution.py:326
  27.0 38.4 %collective-permute-start.25 = (bf16[128,1024]{1,0:T(8,128)(2,1)}, bf16[128,1024]{1,0:T(8,128)(2,1)}, u32[]{:S(2)}, u32[]{:S(2)}) collective-permute-start(bf16[128,1024]{1,0:T(8,128)(2,1)} %param.29), channel_id=1, source_target_pairs={{0,4},{4,0},{1,5},{5,1},{2,6},{6,2},{3,7},{7,3},{8,12},{12,8},{9,1... | collective-permute-start | bytes 786440 | tf_op jit(solution)/shard_map/ppermute | solution.py:326
  60.2 43.3 %collective-permute-start.15 = (bf16[512,1024]{1,0:T(8,128)(2,1)S(1)}, bf16[512,1024]{1,0:T(8,128)(2,1)S(1)}, u32[]{:S(2)}, u32[]{:S(2)}) collective-permute-start(bf16[512,1024]{1,0:T(8,128)(2,1)S(1)} %dynamic-slice_bitcast_fusion), channel_id=1, source_target_pairs={{0,0},{4,1},{2,2},{6,3},{1,4},{5,5},{3,6},{7,7},{8,8},{12,9},{10,1... | collective-permute-start | bytes 3145736 | tf_op jit(solution)/shard_map/ppermute | solution.py:355
  89.5 134.0 %collective-permute-start.29 = (bf16[256,1024]{1,0:T(8,128)(2,1)}, bf16[256,1024]{1,0:T(8,128)(2,1)}, u32[]{:S(2)}, u32[]{:S(2)}) collective-permute-start(bf16[256,1024]{1,0:T(8,128)(2,1)} %get-tuple-element.72), channel_id=1, source_target_pairs={{0,2},{1,3},{2,0},{3,1},{4,6},{5,7},{6,4},{7,5},{8,10},{9,11},{10,... | collective-permute-start | bytes 1572872 | tf_op jit(solution)/shard_map/ppermute | solution.py:326
  103.4 32.7 %collective-permute-start.9 = (bf16[256,1024]{1,0:T(8,128)(2,1)S(1)}, bf16[256,1024]{1,0:T(8,128)(2,1)S(1)}, u32[]{:S(2)}, u32[]{:S(2)}) collective-permute-start(bf16[256,1024]{1,0:T(8,128)(2,1)S(1)} %constant_dynamic-update-slice_fusion.25), channel_id=1, source_target_pairs={{0,2},{1,3},{2,0},{3,1},{4,6},{5,7},{6,4},{7,5},{8,10},{9,11},{10,... | collective-permute-start | bytes 1572872 | tf_op jit(solution)/shard_map/ppermute | solution.py:326
  103.5 29.6 %collective-permute-start.20 = (bf16[256,1024]{1,0:T(8,128)(2,1)S(1)}, bf16[256,1024]{1,0:T(8,128)(2,1)S(1)}, u32[]{:S(2)}, u32[]{:S(2)}) collective-permute-start(bf16[256,1024]{1,0:T(8,128)(2,1)S(1)} %collective-permute-done.19), channel_id=1, source_target_pairs={{0,4},{4,0},{1,5},{5,1},{2,6},{6,2},{3,7},{7,3},{8,12},{12,8},{9,1... | collective-permute-start | bytes 1572872 | tf_op jit(solution)/shard_map/ppermute | solution.py:326
  104.8 31.4 %collective-permute-start.21 = (bf16[256,1024]{1,0:T(8,128)(2,1)S(1)}, bf16[256,1024]{1,0:T(8,128)(2,1)}, u32[]{:S(2)}, u32[]{:S(2)}) collective-permute-start(bf16[256,1024]{1,0:T(8,128)(2,1)S(1)} %collective-permute-done.19), channel_id=1, source_target_pairs={{0,8},{8,16},{16,24},{24,0},{1,9},{9,17},{17,25},{25,1},{2,10},{10... | collective-permute-start | bytes 1572872 | tf_op jit(solution)/shard_map/ppermute | solution.py:326
  133.1 65.5 %collective-permute-start.16 = (bf16[512,1024]{1,0:T(8,128)(2,1)S(1)}, bf16[512,1024]{1,0:T(8,128)(2,1)}, u32[]{:S(2)}, u32[]{:S(2)}) collective-permute-start(bf16[512,1024]{1,0:T(8,128)(2,1)S(1)} %constant_dynamic-update-slice_fusion.83), channel_id=1, source_target_pairs={{0,1},{1,0},{2,3},{3,2},{4,5},{5,4},{6,7},{7,6},{8,9},{9,8},{10,11... | collective-permute-start | bytes 3145736 | tf_op jit(solution)/shard_map/ppermute | solution.py:329
  142.0 51.0 %collective-permute-start.22 = (bf16[256,1024]{1,0:T(8,128)(2,1)}, bf16[256,1024]{1,0:T(8,128)(2,1)}, u32[]{:S(2)}, u32[]{:S(2)}) collective-permute-start(bf16[256,1024]{1,0:T(8,128)(2,1)} %collective-permute-done.21), channel_id=1, source_target_pairs={{0,4},{4,0},{1,5},{5,1},{2,6},{6,2},{3,7},{7,3},{8,12},{12,8},{9,1... | collective-permute-start | bytes 1572872 | tf_op jit(solution)/shard_map/ppermute | solution.py:326
  149.7 45.1 %collective-permute-start.23 = (bf16[256,1024]{1,0:T(8,128)(2,1)}, bf16[256,1024]{1,0:T(8,128)(2,1)}, u32[]{:S(2)}, u32[]{:S(2)}) collective-permute-start(bf16[256,1024]{1,0:T(8,128)(2,1)} %collective-permute-done.21), channel_id=1, source_target_pairs={{0,8},{8,16},{16,24},{24,0},{1,9},{9,17},{17,25},{25,1},{2,10},{10... | collective-permute-start | bytes 1572872 | tf_op jit(solution)/shard_map/ppermute | solution.py:326
  150.9 38.8 %collective-permute-start.28 = (bf16[256,1024]{1,0:T(8,128)(2,1)}, bf16[256,1024]{1,0:T(8,128)(2,1)}, u32[]{:S(2)}, u32[]{:S(2)}) collective-permute-start(bf16[256,1024]{1,0:T(8,128)(2,1)} %collective-permute-done.27), channel_id=1, source_target_pairs={{0,8},{8,16},{16,24},{24,0},{1,9},{9,17},{17,25},{25,1},{2,10},{10... | collective-permute-start | bytes 1572872 | tf_op jit(solution)/shard_map/ppermute | solution.py:326
  193.0 30.5 %collective-permute-start.30 = (bf16[256,1024]{1,0:T(8,128)(2,1)}, bf16[256,1024]{1,0:T(8,128)(2,1)}, u32[]{:S(2)}, u32[]{:S(2)}) collective-permute-start(bf16[256,1024]{1,0:T(8,128)(2,1)} %collective-permute-done.26), channel_id=1, source_target_pairs={{0,2},{1,3},{2,0},{3,1},{4,6},{5,7},{6,4},{7,5},{8,10},{9,11},{10,... | collective-permute-start | bytes 1572872 | tf_op jit(solution)/shard_map/ppermute | solution.py:326
  194.9 28.7 %collective-permute-start.31 = (bf16[256,1024]{1,0:T(8,128)(2,1)}, bf16[256,1024]{1,0:T(8,128)(2,1)}, u32[]{:S(2)}, u32[]{:S(2)}) collective-permute-start(bf16[256,1024]{1,0:T(8,128)(2,1)} %collective-permute-done.27), channel_id=1, source_target_pairs={{0,2},{1,3},{2,0},{3,1},{4,6},{5,7},{6,4},{7,5},{8,10},{9,11},{10,... | collective-permute-start | bytes 1572872 | tf_op jit(solution)/shard_map/ppermute | solution.py:326
  342.7 62.6 %collective-permute-start.42 = (f32[512,1024]{1,0:T(8,128)}, f32[512,1024]{1,0:T(8,128)}, u32[]{:S(2)}, u32[]{:S(2)}) collective-permute-start(f32[512,1024]{1,0:T(8,128)} %slice.562), channel_id=1, source_target_pairs={{0,1},{1,0},{2,3},{3,2},{4,5},{5,4},{6,7},{7,6},{8,9},{9,8},{10,11... | collective-permute-start | bytes 6291464 | tf_op jit(solution)/shard_map/ppermute | solution.py:329
  357.6 41.6 %collective-permute-start.35 = (bf16[512,1024]{1,0:T(8,128)(2,1)}, bf16[512,1024]{1,0:T(8,128)(2,1)}, u32[]{:S(2)}, u32[]{:S(2)}) collective-permute-start(bf16[512,1024]{1,0:T(8,128)(2,1)} %constant_dynamic-update-slice_fusion.116), channel_id=1, source_target_pairs={{0,0},{1,4},{2,2},{3,6},{4,1},{5,5},{6,3},{7,7},{8,8},{9,12},{10,1... | collective-permute-start | bytes 3145736 | tf_op jit(solution)/shard_map/ppermute | solution.py:567
  361.6 43.0 %collective-permute-start.37 = (bf16[512,1024]{1,0:T(8,128)(2,1)}, bf16[512,1024]{1,0:T(8,128)(2,1)S(1)}, u32[]{:S(2)}, u32[]{:S(2)}) collective-permute-start(bf16[512,1024]{1,0:T(8,128)(2,1)} %constant_dynamic-update-slice_fusion.116), channel_id=1, source_target_pairs={{0,2},{1,6},{2,0},{3,4},{4,3},{5,7},{6,1},{7,5},{8,10},{9,14},{10,... | collective-permute-start | bytes 3145736 | tf_op jit(solution)/shard_map/ppermute | solution.py:567
  364.0 41.2 %collective-permute-start.55 = (bf16[4,16,6144]{2,1,0:T(8,128)(2,1)S(1)}, bf16[4,16,6144]{2,1,0:T(8,128)(2,1)}, u32[]{:S(2)}, u32[]{:S(2)}) collective-permute-start(bf16[4,16,6144]{2,1,0:T(8,128)(2,1)S(1)} %pad_maximum_fusion.12), channel_id=1, source_target_pairs={{0,8},{8,16},{16,24},{24,0},{1,9},{9,17},{17,25},{25,1},{2,10},{10... | collective-permute-start | bytes 2359304 | tf_op jit(solution)/shard_map/ppermute | solution.py:326
  399.2 27.0 %collective-permute-start.36 = (bf16[512,1024]{1,0:T(8,128)(2,1)}, bf16[512,1024]{1,0:T(8,128)(2,1)S(1)}, u32[]{:S(2)}, u32[]{:S(2)}) collective-permute-start(bf16[512,1024]{1,0:T(8,128)(2,1)} %collective-permute-done.35), channel_id=1, source_target_pairs={{0,1},{1,0},{2,3},{3,2},{4,5},{5,4},{6,7},{7,6},{8,9},{9,8},{10,11... | collective-permute-start | bytes 3145736 | tf_op jit(solution)/shard_map/ppermute | solution.py:329
  411.0 27.6 %collective-permute-start.44 = (bf16[512,1024]{1,0:T(8,128)(2,1)S(1)}, bf16[512,1024]{1,0:T(8,128)(2,1)}, u32[]{:S(2)}, u32[]{:S(2)}) collective-permute-start(bf16[512,1024]{1,0:T(8,128)(2,1)S(1)} %constant_dynamic-update-slice_fusion.124), channel_id=1, source_target_pairs={{0,0},{1,4},{2,2},{3,6},{4,1},{5,5},{6,3},{7,7},{8,8},{9,12},{10,1... | collective-permute-start | bytes 3145736 | tf_op jit(solution)/shard_map/ppermute | solution.py:567
  438.6 32.7 %collective-permute-start.45 = (bf16[512,1024]{1,0:T(8,128)(2,1)}, bf16[512,1024]{1,0:T(8,128)(2,1)}, u32[]{:S(2)}, u32[]{:S(2)}) collective-permute-start(bf16[512,1024]{1,0:T(8,128)(2,1)} %collective-permute-done.44), channel_id=1, source_target_pairs={{0,1},{1,0},{2,3},{3,2},{4,5},{5,4},{6,7},{7,6},{8,9},{9,8},{10,11... | collective-permute-start | bytes 3145736 | tf_op jit(solution)/shard_map/ppermute | solution.py:329
  438.6 35.7 %collective-permute-start.47 = (bf16[512,1024]{1,0:T(8,128)(2,1)}, bf16[512,1024]{1,0:T(8,128)(2,1)}, u32[]{:S(2)}, u32[]{:S(2)}) collective-permute-start(bf16[512,1024]{1,0:T(8,128)(2,1)} %collective-permute-done.46), channel_id=1, source_target_pairs={{0,1},{1,0},{2,3},{3,2},{4,5},{5,4},{6,7},{7,6},{8,9},{9,8},{10,11... | collective-permute-start | bytes 3145736 | tf_op jit(solution)/shard_map/ppermute | solution.py:329
  (129 other events, 2294.4 us)
